TPU v7x, 256 devices: a whole 4x4x8 slice. The times are simulated.
256 devices in a mesh: leaf: 64 (over z, y, core), off: 4 (over x).
Axes of the slice: x: 4, y: 4, z: 8, core: 2. Of those that a mesh axis runs over, the one named last changes fastest.
Arguments:
- multipoles: bfloat16 [65536, 488], P('leaf'), may hold values from -6 to 6
- kernels: bfloat16 [40, 488, 488], P('off'), may hold values from -0.0390625 to 0.0390625
- transfer: bfloat16 [8, 488, 488], replicated, may hold values from -0.09375 to 0.09375
- leaf_target: int32 [64, 40, 1024], P('leaf', 'off'), may hold values from 0 to 1023, as said below
- leaf_source: int32 [64, 40, 1024], P('leaf', 'off'), may hold values from 0 to 1407
- leaf_count: int32 [64, 40], P('leaf', 'off'), may hold values from 512 to 1024
- coarse_target: int32 [64, 40, 128], P('leaf', 'off'), may hold values from 0 to 127, as said below
- coarse_source: int32 [64, 40, 128], P('leaf', 'off'), may hold values from 0 to 223
- coarse_count: int32 [64, 40], P('leaf', 'off'), may hold values from 64 to 128
- ghost_send: int32 [64, 6, 64], P('leaf'), may hold values from 0 to 1343, as said below
- coarse_send: int32 [64, 6, 16], P('leaf'), may hold values from 0 to 207, as said below
Outputs:
- expansions: float32 [65536, 488], P(('leaf', 'off'))
Inputs may be any that keep to these rules, and one draw needn't show every extreme that they name: Per partition and class, leaf_target is a permutation of 0 to 1023. Per partition and class, coarse_target is a permutation of 0 to 127. `ghost_send`: in round b every index is below 1024 + b * 64. `coarse_send`: in round b every index is below 128 + b * 16.
All inputs are finite; a program needn't handle non-finite values.
Results may differ from a plain program's by a relative error of at most 0.0009.
Values may be sent and summed in bfloat16 or wider, within the bound.
A program may use at most 64 MiB of HBM per device.

v0:
```python
import functools

import jax
import jax.numpy as jnp
from jax import lax
from jax.experimental import pallas as pl
from jax.experimental.pallas import tpu as pltpu
from jax.sharding import PartitionSpec as P


def partner(block, axis, apart):
    count = lax.axis_size(axis)
    route = []
    for low in range(count):
        high = low | 1 << apart
        if high != low and high < count:
            route += [(low, high), (high, low)]
    return lax.ppermute(block, axis, route)


def slot_table(target, source, pair_count, pad_row):
    pair = lax.broadcasted_iota(jnp.int32, target.shape, 1)
    payload = jnp.where(pair < pair_count[:, None], source, pad_row)
    _, slot = lax.sort((target, payload), dimension=1, num_keys=1)
    return slot


def translate_kernel(spread, slot_ref, buf_ref, k_ref, *rest):
    if spread:
        high_ref, low_ref, t_ref, out_ref = rest
        nt = (((1,), (1,)), ((), ()))
        out_ref[...] = lax.dot_general(
            high_ref[...], t_ref[...], nt, preferred_element_type=jnp.float32
        ) + lax.dot_general(low_ref[...], t_ref[...], nt, preferred_element_type=jnp.float32)
    else:
        (out_ref,) = rest
        out_ref[...] = jnp.zeros(out_ref.shape, out_ref.dtype)
    rows = buf_ref.shape[0]
    tile = out_ref.shape[0]

    def one_class(c, carry):
        ids = slot_ref[c]
        hot = (ids == lax.broadcasted_iota(jnp.int32, (tile, rows), 1)).astype(buf_ref.dtype)
        picked = jnp.dot(hot, buf_ref[...], preferred_element_type=jnp.float32)
        out_ref[...] += jnp.dot(
            picked.astype(k_ref.dtype), k_ref[c], preferred_element_type=jnp.float32
        )
        return carry

    lax.fori_loop(0, k_ref.shape[0], one_class, 0)


def translate(slot, buffer, kernels, spread=None):
    groups, classes, tile, _ = slot.shape
    rows, width = buffer.shape
    in_specs = [
        pl.BlockSpec((None, classes, tile, 1), lambda g: (g, 0, 0, 0)),
        pl.BlockSpec((rows, width), lambda g: (0, 0)),
        pl.BlockSpec((classes, width, width), lambda g: (0, 0, 0)),
    ]
    operands = [slot, buffer, kernels]
    if spread is not None:
        high, low, transfer = spread
        in_specs += [
            pl.BlockSpec((tile, width), lambda g: (0, 0)),
            pl.BlockSpec((tile, width), lambda g: (0, 0)),
            pl.BlockSpec((None, width, width), lambda g: (g, 0, 0)),
        ]
        operands += [high, low, transfer]
    flops = 2 * groups * classes * tile * width * (rows + width)
    return pl.pallas_call(
        functools.partial(translate_kernel, spread is not None),
        grid=(groups,),
        in_specs=in_specs,
        out_specs=pl.BlockSpec((None, tile, width), lambda g: (g, 0, 0)),
        out_shape=jax.ShapeDtypeStruct((groups, tile, width), jnp.float32),
        compiler_params=pltpu.CompilerParams(vmem_limit_bytes=48 * 1024 * 1024),
        cost_estimate=pl.CostEstimate(
            flops=flops, bytes_accessed=2 * kernels.size + 2 * buffer.size, transcendentals=0
        ),
    )(*operands)


def on_device(
    multipoles,
    kernels,
    transfer,
    leaf_target,
    leaf_source,
    leaf_count,
    coarse_target,
    coarse_source,
    coarse_count,
    ghost_send,
    coarse_send,
):
    width = multipoles.shape[1]
    rounds = lax.axis_size("leaf").bit_length() - 1
    boxes = multipoles.shape[0]
    parents = boxes // 8
    classes = kernels.shape[0]
    leaf_ghost = ghost_send.shape[2]
    coarse_ghost = coarse_send.shape[2]
    leaf_rows = boxes + rounds * leaf_ghost
    coarse_rows = parents + rounds * coarse_ghost

    parent = jnp.dot(
        multipoles.reshape(-1, 8 * width),
        transfer.reshape(8 * width, width),
        preferred_element_type=jnp.float32,
    ).astype(jnp.bfloat16)

    leaf_slot = slot_table(leaf_target[0], leaf_source[0], leaf_count[0], leaf_rows)
    coarse_slot = slot_table(coarse_target[0], coarse_source[0], coarse_count[0], coarse_rows)
    leaf_slot = leaf_slot.reshape(classes, parents, 8).transpose(2, 0, 1)[..., None]
    coarse_slot = coarse_slot[None, :, :, None]

    buffer = jnp.zeros((leaf_rows, width), multipoles.dtype)
    buffer = lax.dynamic_update_slice(buffer, multipoles, (0, 0))
    coarse_buffer = jnp.zeros((coarse_rows, width), parent.dtype)
    coarse_buffer = lax.dynamic_update_slice(coarse_buffer, parent, (0, 0))
    for bit_index in range(rounds):
        outgoing = jnp.concatenate(
            [buffer[ghost_send[0, bit_index]], coarse_buffer[coarse_send[0, bit_index]]], axis=0
        )
        arrived = partner(outgoing, "leaf", bit_index)
        buffer = lax.dynamic_update_slice(
            buffer, arrived[:leaf_ghost], (boxes + bit_index * leaf_ghost, 0)
        )
        coarse_buffer = lax.dynamic_update_slice(
            coarse_buffer, arrived[leaf_ghost:], (parents + bit_index * coarse_ghost, 0)
        )

    coarse_local = 0.5 * translate(coarse_slot, coarse_buffer, kernels)[0]
    coarse_high = coarse_local.astype(jnp.bfloat16)
    coarse_low = (coarse_local - coarse_high.astype(jnp.float32)).astype(jnp.bfloat16)
    partial_sum = translate(leaf_slot, buffer, kernels, (coarse_high, coarse_low, transfer))
    mine = lax.psum_scatter(partial_sum, "off", scatter_dimension=1, tiled=True)
    return mine.transpose(1, 0, 2).reshape(-1, width)


def solution(mesh):
    in_specs = (
        P("leaf", None),
        P("off", None, None),
        P(),
        P("leaf", "off", None),
        P("leaf", "off", None),
        P("leaf", "off"),
        P("leaf", "off", None),
        P("leaf", "off", None),
        P("leaf", "off"),
        P("leaf", None, None),
        P("leaf", None, None),
    )
    out_specs = P(("leaf", "off"), None)
    return jax.shard_map(
        on_device, mesh=mesh, in_specs=in_specs, out_specs=out_specs, check_vma=False
    )
```

profile of v0, /device:TPU:16, one launch (start us, length us, event | category | flops | bytes accessed | tf_op | source)
XLA Modules:
  0.0 171.8 jit_solution(13290359794162039966)
XLA Ops:
  6.5 0.7 fusion.11
  7.3 0.7 fusion.12
  8.0 1.5 copy.23
  9.5 1.8 %reshape.353 = bf16[128,3904]{1,0:T(8,128)(2,1)S(1)} reshape(bf16[1024,488]{1,0:T(8,128)(2,1)S(1)} %copy.23) | data formatting | bytes 1998848 | tf_op jit(solution)/shard_map/reshape | solution.py:108
  11.3 3.8 %convolution_convert_fusion = bf16[128,488]{0,1:T(8,128)(2,1)S(1)} fusion(bf16[128,3904]{1,0:T(8,128)(2,1)S(1)} %reshape.353, bf16[3904,488]{1,0:T(8,128)(2,1)} %bitcast.78), kind=kOutput, calls=%fused_computation.12 | convolution fusion | flops 487781376 | bytes 4934656 | tf_op jit(solution)/shard_map/dot_general | solution.py:107
  15.2 0.1 copy.25
  15.4 0.1 dynamic_update_slice.42
  15.5 0.6 gather_fusion.1
  16.1 0.7 gather_fusion
  16.9 0.1 collective-permute-start
  17.0 0.6 copy.43
  17.6 0.7 bitcast_select_fusion.1
  18.2 0.0 sort.35.cloned.1.call-update
  18.3 0.0 sort.33.cloned.1.call-start
  18.4 0.6 gather_fusion.3
  19.0 0.7 gather_fusion.2
  19.7 1.4 collective-permute-start.1
  21.1 3.5 %collective-permute-done.1 = bf16[80,488]{1,0:T(8,128)(2,1)S(1)} collective-permute-done((bf16[80,488]{1,0:T(8,128)(2,1)S(1)}, bf16[80,488]{1,0:T(8,128)(2,1)S(1)}, u32[]{:S(2)}, u32[]{:S(2)}) %collective-permute-start.1) | collective-permute-done | bytes 78112 | tf_op jit(solution)/shard_map/ppermute | solution.py:18
  24.7 0.6 gather_fusion.5
  25.3 0.7 gather_fusion.4
  26.0 2.2 %collective-permute-start.2 = (bf16[80,488]{1,0:T(8,128)(2,1)S(1)}, bf16[80,488]{1,0:T(8,128)(2,1)S(1)}, u32[]{:S(2)}, u32[]{:S(2)}) collective-permute-start(bf16[80,488]{1,0:T(8,128)(2,1)S(1)} %pad_maximum_fusion.2), channel_id=1, source_target_pairs={{0,16},{16,0},{4,20},{20,4},{8,24},{24,8},{12,28},{28,12},{32,48},... | collective-permute-start | bytes 234248 | tf_op jit(solution)/shard_map/ppermute | solution.py:18
  28.2 3.9 %collective-permute-done.2 = bf16[80,488]{1,0:T(8,128)(2,1)S(1)} collective-permute-done((bf16[80,488]{1,0:T(8,128)(2,1)S(1)}, bf16[80,488]{1,0:T(8,128)(2,1)S(1)}, u32[]{:S(2)}, u32[]{:S(2)}) %collective-permute-start.2) | collective-permute-done | bytes 78112 | tf_op jit(solution)/shard_map/ppermute | solution.py:18
  32.0 0.6 gather_fusion.7
  32.7 0.7 gather_fusion.6
  33.4 2.0 %collective-permute-start.3 = (bf16[80,488]{1,0:T(8,128)(2,1)S(1)}, bf16[80,488]{1,0:T(8,128)(2,1)S(1)}, u32[]{:S(2)}, u32[]{:S(2)}) collective-permute-start(bf16[80,488]{1,0:T(8,128)(2,1)S(1)} %pad_maximum_fusion.3), channel_id=1, source_target_pairs={{0,32},{32,0},{4,36},{36,4},{8,40},{40,8},{12,44},{44,12},{16,48},... | collective-permute-start | bytes 234248 | tf_op jit(solution)/shard_map/ppermute | solution.py:18
  35.4 2.5 %collective-permute-done.3 = bf16[80,488]{1,0:T(8,128)(2,1)S(1)} collective-permute-done((bf16[80,488]{1,0:T(8,128)(2,1)S(1)}, bf16[80,488]{1,0:T(8,128)(2,1)S(1)}, u32[]{:S(2)}, u32[]{:S(2)}) %collective-permute-start.3) | collective-permute-done | bytes 78112 | tf_op jit(solution)/shard_map/ppermute | solution.py:18
  37.9 0.6 gather_fusion.9
  38.5 0.7 gather_fusion.8
  39.3 3.4 %collective-permute-start.4 = (bf16[80,488]{1,0:T(8,128)(2,1)S(1)}, bf16[80,488]{1,0:T(8,128)(2,1)S(1)}, u32[]{:S(2)}, u32[]{:S(2)}) collective-permute-start(bf16[80,488]{1,0:T(8,128)(2,1)S(1)} %pad_maximum_fusion.4), channel_id=1, source_target_pairs={{0,64},{64,0},{4,68},{68,4},{8,72},{72,8},{12,76},{76,12},{16,80},... | collective-permute-start | bytes 234248 | tf_op jit(solution)/shard_map/ppermute | solution.py:18
  42.6 2.4 %collective-permute-done.4 = bf16[80,488]{1,0:T(8,128)(2,1)S(1)} collective-permute-done((bf16[80,488]{1,0:T(8,128)(2,1)S(1)}, bf16[80,488]{1,0:T(8,128)(2,1)S(1)}, u32[]{:S(2)}, u32[]{:S(2)}) %collective-permute-start.4) | collective-permute-done | bytes 78112 | tf_op jit(solution)/shard_map/ppermute | solution.py:18
  45.0 0.6 gather_fusion.11
  45.6 0.7 gather_fusion.10
  46.4 7.8 %collective-permute-start.5 = (bf16[80,488]{1,0:T(8,128)(2,1)S(1)}, bf16[80,488]{1,0:T(8,128)(2,1)S(1)}, u32[]{:S(2)}, u32[]{:S(2)}) collective-permute-start(bf16[80,488]{1,0:T(8,128)(2,1)S(1)} %pad_maximum_fusion.5), channel_id=1, source_target_pairs={{0,128},{128,0},{4,132},{132,4},{8,136},{136,8},{12,140},{140,12},... | collective-permute-start | bytes 234248 | tf_op jit(solution)/shard_map/ppermute | solution.py:18
  54.2 0.7 bitcast_select_fusion
  54.9 0.6 copy.42
  55.5 0.0 sort.33.cloned.1.call-update
  55.5 0.2 reduce-scatter.2.cloned.1.call-start
  55.8 0.0 sort.35.cloned.1.call-done
  55.8 0.9 copy.26.slot_ref
  56.8 3.6 %sort.33.cloned.1.call-done = (s32[10,1024]{1,0:T(8,128)}, s32[10,1024]{1,0:T(8,128)}) async-done(((s32[10,1024]{1,0:T(8,128)}, s32[10,1024]{1,0:T(8,128)}), (s32[10,1024]{1,0:T(8,128)}, s32[10,1024]{1,0:T(8,128)})) %sort.33.cloned.1.call-update) | async-done | bytes 81936 | tf_op jit(solution)/shard_map/sort | solution.py:24
  60.4 1.2 reshape.352
  61.6 9.2 %copy.27.slot_ref = s32[8,10,128,1]{3,2,1,0:T(8,128)} copy(s32[8,10,128,1]{0,2,1,3:T(8,128)S(1)} %bitcast.79) | data formatting | bytes 81920 | tf_op jit(solution)/shard_map/broadcast_in_dim | solution.py:115
  70.8 2.4 %copy-done = bf16[10,488,488]{2,1,0:T(8,128)(2,1)S(1)} copy-done((bf16[10,488,488]{2,1,0:T(8,128)(2,1)S(1)}, bf16[10,488,488]{2,1,0:T(8,128)(2,1)}, u32[]{:S(2)}) %copy-start) | copy-done | bytes 4762904
  73.2 4.0 %shard_map.109 = f32[1,128,488]{2,1,0:T(8,128)S(1)} custom-call(s32[1,10,128,1]{3,2,1,0:T(8,128)S(1)} %copy.26.slot_ref, bf16[224,488]{1,0:T(8,128)(2,1)S(1)} %slice_dynamic-update-slice_fusion.6.buf_ref, bf16[10,488,488]{2,1,0:T(8,128)(2,1)S(1)} %copy-done), custom_call_target="tpu_custom_call" | custom-call | flops 889487360 | bytes 4981504 | tf_op jit(solution)/shard_map/pallas_call | solution.py:71
  77.3 55.7 %shard_map.110 = f32[8,128,488]{2,1,0:T(8,128)} custom-call(s32[8,10,128,1]{3,2,1,0:T(8,128)} %copy.27.slot_ref, bf16[1408,488]{1,0:T(8,128)(2,1)S(1)} %slice_dynamic-update-slice_fusion.buf_ref, bf16[10,488,488]{2,1,0:T(8,128)(2,1)} %k_ref.3, bf16[128,488]{1,0:T(8,128)(2,1)S(1)} %bitcast_convert_fusion.rest_0_, bf16[128,488]{1,0:T(8,128)(2,1)S(1)} %fusion.rest_1_, ...), custom_call_target="tpu_custom_call" | custom-call | flops 18949079040 | bytes 6137088 | tf_op jit(solution)/shard_map/pallas_call | solution.py:71
  133.0 30.0 %reduce-scatter.2.cloned.1.call-done = f32[8,32,488]{2,1,0:T(8,128)} async-done(((f32[8,128,488]{2,1,0:T(8,128)}), f32[8,32,488]{2,1,0:T(8,128)}) %reduce-scatter.2.cloned.1.call-update) | async-done | bytes 499728 | tf_op jit(solution)/shard_map/reduce_scatter | solution.py:138
  163.0 1.3 copy.41
  164.3 1.0 copy.29
  (50 shorter events, 0.3 us)
Async XLA Ops:
  6.5 49.3 %sort.35.cloned.1.call-start = ((), (), s32[]{:S(2)}) async-start(), calls=%async_computation.3 | async-start | bytes 49184 | tf_op jit(solution)/shard_map/sort | solution.py:24
  15.3 1.6 copy-start.4
  15.3 2.2 %copy-start.3 = (s32[1,10,128]{2,0,1:T(1,128)S(1)}, s32[1,10,128]{2,0,1:T(1,128)}, u32[]{:S(2)}) copy-start(s32[1,10,128]{2,0,1:T(1,128)} %param.18) | copy-start | bytes 15364
  15.3 2.2 %copy-start.6 = (s32[1,10]{1,0:T(1,128)S(1)}, s32[1,10]{1,0:T(1,128)}, u32[]{:S(2)}) copy-start(s32[1,10]{1,0:T(1,128)} %param.19) | copy-start | bytes 124
  16.9 1.5 collective-permute-start
  18.3 42.1 %sort.33.cloned.1.call-start = ((), (), s32[]{:S(2)}) async-start(), calls=%async_computation.2 | async-start | bytes 393248 | tf_op jit(solution)/shard_map/sort | solution.py:24
  19.7 4.9 %collective-permute-start.1 = (bf16[80,488]{1,0:T(8,128)(2,1)S(1)}, bf16[80,488]{1,0:T(8,128)(2,1)S(1)}, u32[]{:S(2)}, u32[]{:S(2)}) collective-permute-start(bf16[80,488]{1,0:T(8,128)(2,1)S(1)} %pad_maximum_fusion.1), channel_id=1, source_target_pairs={{0,8},{8,0},{4,12},{12,4},{16,24},{24,16},{20,28},{28,20},{32,40},... | collective-permute-start | bytes 234248 | tf_op jit(solution)/shard_map/ppermute | solution.py:18
  26.0 6.0 %collective-permute-start.2 = (bf16[80,488]{1,0:T(8,128)(2,1)S(1)}, bf16[80,488]{1,0:T(8,128)(2,1)S(1)}, u32[]{:S(2)}, u32[]{:S(2)}) collective-permute-start(bf16[80,488]{1,0:T(8,128)(2,1)S(1)} %pad_maximum_fusion.2), channel_id=1, source_target_pairs={{0,16},{16,0},{4,20},{20,4},{8,24},{24,8},{12,28},{28,12},{32,48},... | collective-permute-start | bytes 234248 | tf_op jit(solution)/shard_map/ppermute | solution.py:18
  32.6 21.5 %copy-start.1 = (s32[1,10,1024]{2,0,1:T(1,128)S(1)}, s32[1,10,1024]{2,0,1:T(1,128)}, u32[]{:S(2)}) copy-start(s32[1,10,1024]{2,0,1:T(1,128)} %param.15) | copy-start | bytes 122884
  32.6 21.5 %copy-start.5 = (s32[1,10]{1,0:T(1,128)S(1)}, s32[1,10]{1,0:T(1,128)}, u32[]{:S(2)}) copy-start(s32[1,10]{1,0:T(1,128)} %param.16) | copy-start | bytes 124
  32.7 22.2 %copy-start.2 = (s32[1,10,1024]{2,0,1:T(1,128)S(1)}, s32[1,10,1024]{2,0,1:T(1,128)}, u32[]{:S(2)}) copy-start(s32[1,10,1024]{2,0,1:T(1,128)} %param.14) | copy-start | bytes 122884
  33.4 4.5 %collective-permute-start.3 = (bf16[80,488]{1,0:T(8,128)(2,1)S(1)}, bf16[80,488]{1,0:T(8,128)(2,1)S(1)}, u32[]{:S(2)}, u32[]{:S(2)}) collective-permute-start(bf16[80,488]{1,0:T(8,128)(2,1)S(1)} %pad_maximum_fusion.3), channel_id=1, source_target_pairs={{0,32},{32,0},{4,36},{36,4},{8,40},{40,8},{12,44},{44,12},{16,48},... | collective-permute-start | bytes 234248 | tf_op jit(solution)/shard_map/ppermute | solution.py:18
  39.3 5.8 %collective-permute-start.4 = (bf16[80,488]{1,0:T(8,128)(2,1)S(1)}, bf16[80,488]{1,0:T(8,128)(2,1)S(1)}, u32[]{:S(2)}, u32[]{:S(2)}) collective-permute-start(bf16[80,488]{1,0:T(8,128)(2,1)S(1)} %pad_maximum_fusion.4), channel_id=1, source_target_pairs={{0,64},{64,0},{4,68},{68,4},{8,72},{72,8},{12,76},{76,12},{16,80},... | collective-permute-start | bytes 234248 | tf_op jit(solution)/shard_map/ppermute | solution.py:18
  46.4 24.4 %collective-permute-start.5 = (bf16[80,488]{1,0:T(8,128)(2,1)S(1)}, bf16[80,488]{1,0:T(8,128)(2,1)S(1)}, u32[]{:S(2)}, u32[]{:S(2)}) collective-permute-start(bf16[80,488]{1,0:T(8,128)(2,1)S(1)} %pad_maximum_fusion.5), channel_id=1, source_target_pairs={{0,128},{128,0},{4,132},{132,4},{8,136},{136,8},{12,140},{140,12},... | collective-permute-start | bytes 234248 | tf_op jit(solution)/shard_map/ppermute | solution.py:18
  55.5 107.4 %reduce-scatter.2.cloned.1.call-start = ((), (), s32[]{:S(2)}) async-start(), calls=%async_computation.1 | async-start | bytes 2621440 | tf_op jit(solution)/shard_map/reduce_scatter | solution.py:138
  70.8 2.4 %copy-start = (bf16[10,488,488]{2,1,0:T(8,128)(2,1)S(1)}, bf16[10,488,488]{2,1,0:T(8,128)(2,1)}, u32[]{:S(2)}) copy-start(bf16[10,488,488]{2,1,0:T(8,128)(2,1)} %k_ref.3) | copy-start | bytes 14288644
Sparse Core Ops, SparseCore 0:
  18.4 2.2 sort.39.cloned.1.call-done
  55.7 4.4 sort.37.cloned.1.call-done
  133.1 29.7 reduce-scatter.1
  (2 shorter events, 0.0 us)
where the time goes:
time: 173 us; the launch traced here: 172 us
  Pallas kernels  59.7 us (35%)
  waiting for transfers between devices  42.3 us (24%)
  local copies, waits for them, and re-layouts  32.5 us (19%)
  starting transfers between devices  17 us (10%)
  between operations  13.5 us (8%)
  matrix products  3.83 us (2%)
  other arithmetic  3.03 us (2%)
    pallas_call x2, Pallas kernels, translate(): pl.pallas_call(functools.partial(translate_kernel, spread is not None), g...  59.7 us
    reduce_scatter x1, waiting for transfers between devices, on_device(): mine = lax.psum_scatter(partial_sum, 'off', scatter_dimension=1, tiled=True)  30 us
    ppermute x6, starting transfers between devices, partner(): return lax.ppermute(block, axis, route)  16.8 us
    ppermute x6, waiting for transfers between devices, partner(): return lax.ppermute(block, axis, route)  12.4 us
    broadcast_in_dim x1, local copies, waits for them, and re-layouts, on_device(): leaf_slot.reshape(classes, parents, 8).transpose(2, 0, 1)[..., None]  9.21 us
    unnamed x19, local copies, waits for them, and re-layouts  5.21 us
    gather x6, local copies, waits for them, and re-layouts, on_device(): buffer[ghost_send[0, bit_index]]  4.21 us
    dot_general x1, matrix products, on_device(): jnp.dot(multipoles.reshape(-1, 8 * width), transfer.reshape(8 * width, wi...  3.83 us
  transfers between devices with their start and end apart: 7, of which 5 were waited for; matrix products, arithmetic and copies ran while one was open for 8% of the time, Pallas kernels for 0%

commit v1 on v0

--- a/solution.py
+++ b/solution.py
@@ -25,55 +25,59 @@
     return slot
 
 
-def translate_kernel(spread, slot_ref, buf_ref, k_ref, *rest):
+def translate_kernel(spread, devices, slot_ref, buf_ref, k_ref, *rest):
     if spread:
         high_ref, low_ref, t_ref, out_ref = rest
         nt = (((1,), (1,)), ((), ()))
-        out_ref[...] = lax.dot_general(
-            high_ref[...], t_ref[...], nt, preferred_element_type=jnp.float32
-        ) + lax.dot_general(low_ref[...], t_ref[...], nt, preferred_element_type=jnp.float32)
+        octants = t_ref.shape[0]
+        span = high_ref.shape[0] // devices
+        for h in range(octants):
+            term = lax.dot_general(
+                high_ref[...], t_ref[h], nt, preferred_element_type=jnp.float32
+            ) + lax.dot_general(low_ref[...], t_ref[h], nt, preferred_element_type=jnp.float32)
+            for d in range(devices):
+                at = (d * octants + h) * span
+                out_ref[at:at + span, :] = term[d * span:(d + 1) * span]
     else:
         (out_ref,) = rest
         out_ref[...] = jnp.zeros(out_ref.shape, out_ref.dtype)
     rows = buf_ref.shape[0]
     tile = out_ref.shape[0]
-
-    def one_class(c, carry):
-        ids = slot_ref[c]
+    columns = jnp.transpose(slot_ref[...])
+    for c in range(k_ref.shape[0]):
+        ids = columns[:, c:c + 1]
         hot = (ids == lax.broadcasted_iota(jnp.int32, (tile, rows), 1)).astype(buf_ref.dtype)
         picked = jnp.dot(hot, buf_ref[...], preferred_element_type=jnp.float32)
         out_ref[...] += jnp.dot(
             picked.astype(k_ref.dtype), k_ref[c], preferred_element_type=jnp.float32
         )
-        return carry
-
-    lax.fori_loop(0, k_ref.shape[0], one_class, 0)
 
 
-def translate(slot, buffer, kernels, spread=None):
-    groups, classes, tile, _ = slot.shape
+def translate(slot, buffer, kernels, chunk, tile, spread=None, devices=1):
+    classes = kernels.shape[0]
     rows, width = buffer.shape
     in_specs = [
-        pl.BlockSpec((None, classes, tile, 1), lambda g: (g, 0, 0, 0)),
+        pl.BlockSpec((slot.shape[0], tile), lambda g: (0, chunk)),
         pl.BlockSpec((rows, width), lambda g: (0, 0)),
         pl.BlockSpec((classes, width, width), lambda g: (0, 0, 0)),
     ]
     operands = [slot, buffer, kernels]
     if spread is not None:
         high, low, transfer = spread
+        octants = tile // high.shape[0]
         in_specs += [
-            pl.BlockSpec((tile, width), lambda g: (0, 0)),
-            pl.BlockSpec((tile, width), lambda g: (0, 0)),
-            pl.BlockSpec((None, width, width), lambda g: (g, 0, 0)),
+            pl.BlockSpec(high.shape, lambda g: (0, 0)),
+            pl.BlockSpec(low.shape, lambda g: (0, 0)),
+            pl.BlockSpec((octants, width, width), lambda g: (chunk, 0, 0)),
         ]
         operands += [high, low, transfer]
-    flops = 2 * groups * classes * tile * width * (rows + width)
+    flops = 2 * classes * tile * width * (rows + width)
     return pl.pallas_call(
-        functools.partial(translate_kernel, spread is not None),
-        grid=(groups,),
+        functools.partial(translate_kernel, spread is not None, devices),
+        grid=(1,),
         in_specs=in_specs,
-        out_specs=pl.BlockSpec((None, tile, width), lambda g: (g, 0, 0)),
-        out_shape=jax.ShapeDtypeStruct((groups, tile, width), jnp.float32),
+        out_specs=pl.BlockSpec((tile, width), lambda g: (0, 0)),
+        out_shape=jax.ShapeDtypeStruct((tile, width), jnp.float32),
         compiler_params=pltpu.CompilerParams(vmem_limit_bytes=48 * 1024 * 1024),
         cost_estimate=pl.CostEstimate(
             flops=flops, bytes_accessed=2 * kernels.size + 2 * buffer.size, transcendentals=0
@@ -112,8 +116,13 @@
 
     leaf_slot = slot_table(leaf_target[0], leaf_source[0], leaf_count[0], leaf_rows)
     coarse_slot = slot_table(coarse_target[0], coarse_source[0], coarse_count[0], coarse_rows)
-    leaf_slot = leaf_slot.reshape(classes, parents, 8).transpose(2, 0, 1)[..., None]
-    coarse_slot = coarse_slot[None, :, :, None]
+    chunks = 4
+    devices = lax.axis_size("off")
+    span = parents // devices
+    leaf_slot = leaf_slot.reshape(classes, devices, span, chunks, 8 // chunks)
+    leaf_slot = leaf_slot.transpose(0, 3, 1, 4, 2).reshape(classes, boxes)
+    leaf_slot = jnp.pad(leaf_slot, ((0, 16 - classes), (0, 0)), constant_values=leaf_rows)
+    coarse_slot = jnp.pad(coarse_slot, ((0, 16 - classes), (0, 0)), constant_values=coarse_rows)
 
     buffer = jnp.zeros((leaf_rows, width), multipoles.dtype)
     buffer = lax.dynamic_update_slice(buffer, multipoles, (0, 0))
@@ -131,11 +140,19 @@
             coarse_buffer, arrived[leaf_ghost:], (parents + bit_index * coarse_ghost, 0)
         )
 
-    coarse_local = 0.5 * translate(coarse_slot, coarse_buffer, kernels)[0]
+    coarse_local = 0.5 * translate(coarse_slot, coarse_buffer, kernels, 0, parents)
     coarse_high = coarse_local.astype(jnp.bfloat16)
     coarse_low = (coarse_local - coarse_high.astype(jnp.float32)).astype(jnp.bfloat16)
-    partial_sum = translate(leaf_slot, buffer, kernels, (coarse_high, coarse_low, transfer))
-    mine = lax.psum_scatter(partial_sum, "off", scatter_dimension=1, tiled=True)
+    tile = boxes // chunks
+    mine = []
+    for chunk in range(chunks):
+        partial_sum = translate(
+            leaf_slot, buffer, kernels, chunk, tile, (coarse_high, coarse_low, transfer), devices
+        )
+        if mine:
+            partial_sum, _ = lax.optimization_barrier((partial_sum, mine[-1]))
+        mine.append(lax.psum_scatter(partial_sum, "off", scatter_dimension=0, tiled=True))
+    mine = jnp.stack(mine).reshape(8, span, width)
     return mine.transpose(1, 0, 2).reshape(-1, width)
 
 

time: 173 us -> 187 us (1.081)
  waiting for transfers between devices: 42.3 us -> 80.4 us
  Pallas kernels: 59.7 us -> 44.6 us
  local copies, waits for them, and re-layouts: 32.5 us -> 23.2 us
    reduce_scatter x1 -> x4, waiting for transfers between devices: 30 us -> 68 us  [on_device(): lax.psum_scatter(partial_sum, 'off', scatter_dimension=0, tiled=True)]
    pallas_call x2 -> x5, Pallas kernels: 59.7 us -> 44.6 us  [translate(): pl.pallas_call(functools.partial(translate_kernel, spread is not None, de...]
    broadcast_in_dim x2 -> x0, local copies, waits for them, and re-layouts: 10.2 us -> none  [the longest x1 9.21 us: on_device(): leaf_slot.reshape(classes, parents, 8).transpose(2, 0, 1)[..., None]]
    sort x4 -> x5, local copies, waits for them, and re-layouts: 3.68 us -> 4.96 us  [slot_table(): _, slot = lax.sort((target, payload), dimension=1, num_keys=1)]
    unnamed x19 -> x25, local copies, waits for them, and re-layouts: 5.21 us -> 5.68 us
  transfers between devices with their start and end apart: 7 -> 10, of which waited for: 5 -> 8; matrix products, arithmetic and copies ran while one was open for 8% -> 3% of each run, Pallas kernels for 0% -> 17%
where the time goes in v1:
time: 187 us
  waiting for transfers between devices  80.4 us (43%)
  Pallas kernels  44.6 us (24%)
  local copies, waits for them, and re-layouts  23.2 us (12%)
  starting transfers between devices  17.4 us (9%)
  between operations  13.9 us (7%)
  matrix products  3.83 us (2%)
  other arithmetic  3.28 us (2%)
    reduce_scatter x4, waiting for transfers between devices, on_device(): lax.psum_scatter(partial_sum, 'off', scatter_dimension=0, tiled=True)  68 us
    pallas_call x5, Pallas kernels, translate(): pl.pallas_call(functools.partial(translate_kernel, spread is not None, de...  44.6 us
    ppermute x6, starting transfers between devices, partner(): return lax.ppermute(block, axis, route)  16.8 us
    ppermute x6, waiting for transfers between devices, partner(): return lax.ppermute(block, axis, route)  12.4 us
    unnamed x25, local copies, waits for them, and re-layouts  5.68 us
    sort x5, local copies, waits for them, and re-layouts, slot_table(): _, slot = lax.sort((target, payload), dimension=1, num_keys=1)  4.96 us
    gather x6, local copies, waits for them, and re-layouts, on_device(): buffer[ghost_send[0, bit_index]]  4.21 us
    dot_general x1, matrix products, on_device(): jnp.dot(multipoles.reshape(-1, 8 * width), transfer.reshape(8 * width, wi...  3.83 us
  transfers between devices with their start and end apart: 10, of which 8 were waited for; matrix products, arithmetic and copies ran while one was open for 3% of the time, Pallas kernels for 17%

profile of v1, /device:TPU:16, one launch (start us, length us, event | category | flops | bytes accessed | tf_op | source)
XLA Modules:
  0.0 186.5 jit_solution(14928755512474715384)
XLA Ops:
  6.5 0.7 fusion.11
  7.3 1.5 copy.30
  8.8 1.8 reshape.358
  10.6 3.8 %convolution_convert_fusion = bf16[128,488]{0,1:T(8,128)(2,1)S(1)} fusion(bf16[128,3904]{1,0:T(8,128)(2,1)S(1)} %reshape.358, bf16[3904,488]{1,0:T(8,128)(2,1)} %bitcast.76), kind=kOutput, calls=%fused_computation.12 | convolution fusion | flops 487781376 | bytes 4934656 | tf_op jit(solution)/shard_map/dot_general | solution.py:111
  14.8 0.5 copy-done.7
  15.3 0.6 gather_fusion.1
  15.9 0.7 gather_fusion
  16.7 0.6 copy.46
  17.3 0.7 bitcast_select_fusion.1
  18.1 0.6 gather_fusion.3
  18.7 0.7 gather_fusion.2
  19.5 1.4 collective-permute-start.1
  20.8 3.5 %collective-permute-done.1 = bf16[80,488]{1,0:T(8,128)(2,1)S(1)} collective-permute-done((bf16[80,488]{1,0:T(8,128)(2,1)S(1)}, bf16[80,488]{1,0:T(8,128)(2,1)S(1)}, u32[]{:S(2)}, u32[]{:S(2)}) %collective-permute-start.1) | collective-permute-done | bytes 78112 | tf_op jit(solution)/shard_map/ppermute | solution.py:18
  24.4 0.6 gather_fusion.5
  25.0 0.7 gather_fusion.4
  25.7 2.2 %collective-permute-start.2 = (bf16[80,488]{1,0:T(8,128)(2,1)S(1)}, bf16[80,488]{1,0:T(8,128)(2,1)S(1)}, u32[]{:S(2)}, u32[]{:S(2)}) collective-permute-start(bf16[80,488]{1,0:T(8,128)(2,1)S(1)} %pad_maximum_fusion.3), channel_id=1, source_target_pairs={{0,16},{16,0},{4,20},{20,4},{8,24},{24,8},{12,28},{28,12},{32,48},... | collective-permute-start | bytes 234248 | tf_op jit(solution)/shard_map/ppermute | solution.py:18
  27.9 3.9 %collective-permute-done.2 = bf16[80,488]{1,0:T(8,128)(2,1)S(1)} collective-permute-done((bf16[80,488]{1,0:T(8,128)(2,1)S(1)}, bf16[80,488]{1,0:T(8,128)(2,1)S(1)}, u32[]{:S(2)}, u32[]{:S(2)}) %collective-permute-start.2) | collective-permute-done | bytes 78112 | tf_op jit(solution)/shard_map/ppermute | solution.py:18
  31.8 0.6 gather_fusion.7
  32.4 0.7 gather_fusion.6
  33.1 2.0 %collective-permute-start.3 = (bf16[80,488]{1,0:T(8,128)(2,1)S(1)}, bf16[80,488]{1,0:T(8,128)(2,1)S(1)}, u32[]{:S(2)}, u32[]{:S(2)}) collective-permute-start(bf16[80,488]{1,0:T(8,128)(2,1)S(1)} %pad_maximum_fusion.4), channel_id=1, source_target_pairs={{0,32},{32,0},{4,36},{36,4},{8,40},{40,8},{12,44},{44,12},{16,48},... | collective-permute-start | bytes 234248 | tf_op jit(solution)/shard_map/ppermute | solution.py:18
  35.1 2.5 %collective-permute-done.3 = bf16[80,488]{1,0:T(8,128)(2,1)S(1)} collective-permute-done((bf16[80,488]{1,0:T(8,128)(2,1)S(1)}, bf16[80,488]{1,0:T(8,128)(2,1)S(1)}, u32[]{:S(2)}, u32[]{:S(2)}) %collective-permute-start.3) | collective-permute-done | bytes 78112 | tf_op jit(solution)/shard_map/ppermute | solution.py:18
  37.7 0.6 gather_fusion.9
  38.3 0.7 gather_fusion.8
  39.0 3.4 %collective-permute-start.4 = (bf16[80,488]{1,0:T(8,128)(2,1)S(1)}, bf16[80,488]{1,0:T(8,128)(2,1)S(1)}, u32[]{:S(2)}, u32[]{:S(2)}) collective-permute-start(bf16[80,488]{1,0:T(8,128)(2,1)S(1)} %pad_maximum_fusion.5), channel_id=1, source_target_pairs={{0,64},{64,0},{4,68},{68,4},{8,72},{72,8},{12,76},{76,12},{16,80},... | collective-permute-start | bytes 234248 | tf_op jit(solution)/shard_map/ppermute | solution.py:18
  42.4 2.4 %collective-permute-done.4 = bf16[80,488]{1,0:T(8,128)(2,1)S(1)} collective-permute-done((bf16[80,488]{1,0:T(8,128)(2,1)S(1)}, bf16[80,488]{1,0:T(8,128)(2,1)S(1)}, u32[]{:S(2)}, u32[]{:S(2)}) %collective-permute-start.4) | collective-permute-done | bytes 78112 | tf_op jit(solution)/shard_map/ppermute | solution.py:18
  44.8 0.6 gather_fusion.11
  45.4 0.7 gather_fusion.10
  46.1 7.8 %collective-permute-start.5 = (bf16[80,488]{1,0:T(8,128)(2,1)S(1)}, bf16[80,488]{1,0:T(8,128)(2,1)S(1)}, u32[]{:S(2)}, u32[]{:S(2)}) collective-permute-start(bf16[80,488]{1,0:T(8,128)(2,1)S(1)} %pad_maximum_fusion.6), channel_id=1, source_target_pairs={{0,128},{128,0},{4,132},{132,4},{8,136},{136,8},{12,140},{140,12},... | collective-permute-start | bytes 234248 | tf_op jit(solution)/shard_map/ppermute | solution.py:18
  53.9 0.7 bitcast_select_fusion
  54.6 0.6 copy.45
  55.5 0.7 pad.11.slot_ref
  56.2 3.8 %sort.33.cloned.1.call-done = (s32[10,1024]{1,0:T(8,128)}, s32[10,1024]{1,0:T(8,128)}) async-done(((s32[10,1024]{1,0:T(8,128)}, s32[10,1024]{1,0:T(8,128)}), (s32[10,1024]{1,0:T(8,128)}, s32[10,1024]{1,0:T(8,128)})) %sort.33.cloned.1.call-update) | async-done | bytes 81936 | tf_op jit(solution)/shard_map/sort | solution.py:24
  60.1 1.0 copy.28
  61.1 0.5 copy.29
  61.9 2.4 %copy-done = bf16[10,488,488]{2,1,0:T(8,128)(2,1)S(1)} copy-done((bf16[10,488,488]{2,1,0:T(8,128)(2,1)S(1)}, bf16[10,488,488]{2,1,0:T(8,128)(2,1)}, u32[]{:S(2)}) %copy-start) | copy-done | bytes 4762904
  64.3 2.4 %shard_map.109 = f32[128,488]{1,0:T(8,128)S(1)} custom-call(s32[16,128]{1,0:T(8,128)S(1)} %pad.11.slot_ref, bf16[224,488]{1,0:T(8,128)(2,1)S(1)} %slice_dynamic-update-slice_fusion.6.buf_ref, bf16[10,488,488]{2,1,0:T(8,128)(2,1)S(1)} %copy-done), custom_call_target="tpu_custom_call" | custom-call | flops 889487360 | bytes 4981504 | tf_op jit(solution)/shard_map/pallas_call | solution.py:75
  66.7 10.5 %shard_map.110 = f32[256,488]{1,0:T(8,128)} custom-call(s32[16,1024]{1,0:T(8,128)S(1)} %pad.10.slot_ref, bf16[1408,488]{1,0:T(8,128)(2,1)S(1)} %slice_dynamic-update-slice_fusion.buf_ref, bf16[10,488,488]{2,1,0:T(8,128)(2,1)} %k_ref.9, bf16[128,488]{1,0:T(8,128)(2,1)S(1)} %get-tuple-element.16.rest_0_, bf16[128,488]{1,0:T(8,128)(2,1)S(1)} %get-tuple-element.15.rest_1_, ...), custom_call_target="tpu_custom_call" | custom-call | flops 4737269760 | bytes 6137088 | tf_op jit(solution)/shard_map/pallas_call | solution.py:75
  77.3 10.5 %shard_map.111 = f32[256,488]{1,0:T(8,128)} custom-call(s32[16,1024]{1,0:T(8,128)S(1)} %pad.10.slot_ref, bf16[1408,488]{1,0:T(8,128)(2,1)S(1)} %slice_dynamic-update-slice_fusion.buf_ref, bf16[10,488,488]{2,1,0:T(8,128)(2,1)} %k_ref.9, bf16[128,488]{1,0:T(8,128)(2,1)S(1)} %get-tuple-element.16.rest_0_, bf16[128,488]{1,0:T(8,128)(2,1)S(1)} %get-tuple-element.15.rest_1_, ...), custom_call_target="tpu_custom_call" | custom-call | flops 4737269760 | bytes 6137088 | tf_op jit(solution)/shard_map/pallas_call | solution.py:75
  87.9 11.1 %reduce-scatter.5.cloned.1.call-done = f32[64,488]{1,0:T(8,128)} async-done(((f32[256,488]{1,0:T(8,128)}), f32[64,488]{1,0:T(8,128)}) %reduce-scatter.5.cloned.1.call-update) | async-done | bytes 124944 | tf_op jit(solution)/shard_map/reduce_scatter | solution.py:154
  99.0 0.3 reduce-scatter.9.cloned.1.call-start
  99.3 10.5 %shard_map.112 = f32[256,488]{1,0:T(8,128)} custom-call(s32[16,1024]{1,0:T(8,128)S(1)} %pad.10.slot_ref, bf16[1408,488]{1,0:T(8,128)(2,1)S(1)} %slice_dynamic-update-slice_fusion.buf_ref, bf16[10,488,488]{2,1,0:T(8,128)(2,1)} %k_ref.9, bf16[128,488]{1,0:T(8,128)(2,1)S(1)} %get-tuple-element.16.rest_0_, bf16[128,488]{1,0:T(8,128)(2,1)S(1)} %get-tuple-element.15.rest_1_, ...), custom_call_target="tpu_custom_call" | custom-call | flops 4737269760 | bytes 6137088 | tf_op jit(solution)/shard_map/pallas_call | solution.py:75
  109.8 15.3 %reduce-scatter.7.cloned.1.call-done = f32[64,488]{1,0:T(8,128)} async-done(((f32[256,488]{1,0:T(8,128)}), f32[64,488]{1,0:T(8,128)}) %reduce-scatter.7.cloned.1.call-update) | async-done | bytes 124944 | tf_op jit(solution)/shard_map/reduce_scatter | solution.py:154
  125.2 10.6 %shard_map.113 = f32[256,488]{1,0:T(8,128)} custom-call(s32[16,1024]{1,0:T(8,128)S(1)} %pad.10.slot_ref, bf16[1408,488]{1,0:T(8,128)(2,1)S(1)} %slice_dynamic-update-slice_fusion.buf_ref, bf16[10,488,488]{2,1,0:T(8,128)(2,1)} %k_ref.9, bf16[128,488]{1,0:T(8,128)(2,1)S(1)} %get-tuple-element.16.rest_0_, bf16[128,488]{1,0:T(8,128)(2,1)S(1)} %get-tuple-element.15.rest_1_, ...), custom_call_target="tpu_custom_call" | custom-call | flops 4737269760 | bytes 6137088 | tf_op jit(solution)/shard_map/pallas_call | solution.py:75
  135.8 15.4 %reduce-scatter.9.cloned.1.call-done = f32[64,488]{1,0:T(8,128)} async-done(((f32[256,488]{1,0:T(8,128)}), f32[64,488]{1,0:T(8,128)}) %reduce-scatter.9.cloned.1.call-update) | async-done | bytes 124944 | tf_op jit(solution)/shard_map/reduce_scatter | solution.py:154
  151.3 26.1 %reduce-scatter.11.cloned.1.call-done = f32[64,488]{1,0:T(8,128)} async-done(((f32[256,488]{1,0:T(8,128)}), f32[64,488]{1,0:T(8,128)}) %reduce-scatter.11.cloned.1.call-update) | async-done | bytes 124944 | tf_op jit(solution)/shard_map/reduce_scatter | solution.py:154
  177.4 1.0 pad_maximum_fusion
  178.4 0.3 copy.44
  178.7 1.0 copy.34
  (70 shorter events, 1.4 us)
Async XLA Ops:
  6.5 49.0 %sort.35.cloned.1.call-start = ((), (), s32[]{:S(2)}) async-start(), calls=%async_computation.9 | async-start | bytes 49184 | tf_op jit(solution)/shard_map/sort | solution.py:24
  14.6 0.7 copy-start.7
  14.6 2.1 %copy-start.6 = (s32[1,10,128]{2,0,1:T(1,128)S(1)}, s32[1,10,128]{2,0,1:T(1,128)}, u32[]{:S(2)}) copy-start(s32[1,10,128]{2,0,1:T(1,128)} %param.17) | copy-start | bytes 15364
  14.6 2.7 %copy-start.5 = (s32[1,10,128]{2,0,1:T(1,128)S(1)}, s32[1,10,128]{2,0,1:T(1,128)}, u32[]{:S(2)}) copy-start(s32[1,10,128]{2,0,1:T(1,128)} %param.18) | copy-start | bytes 15364
  14.6 2.7 %copy-start.9 = (s32[1,10]{1,0:T(1,128)S(1)}, s32[1,10]{1,0:T(1,128)}, u32[]{:S(2)}) copy-start(s32[1,10]{1,0:T(1,128)} %param.19) | copy-start | bytes 124
  16.6 1.5 collective-permute-start
  18.0 42.1 %sort.33.cloned.1.call-start = ((), (), s32[]{:S(2)}) async-start(), calls=%async_computation.8 | async-start | bytes 393248 | tf_op jit(solution)/shard_map/sort | solution.py:24
  19.5 4.9 %collective-permute-start.1 = (bf16[80,488]{1,0:T(8,128)(2,1)S(1)}, bf16[80,488]{1,0:T(8,128)(2,1)S(1)}, u32[]{:S(2)}, u32[]{:S(2)}) collective-permute-start(bf16[80,488]{1,0:T(8,128)(2,1)S(1)} %pad_maximum_fusion.2), channel_id=1, source_target_pairs={{0,8},{8,0},{4,12},{12,4},{16,24},{24,16},{20,28},{28,20},{32,40},... | collective-permute-start | bytes 234248 | tf_op jit(solution)/shard_map/ppermute | solution.py:18
  25.7 6.0 %collective-permute-start.2 = (bf16[80,488]{1,0:T(8,128)(2,1)S(1)}, bf16[80,488]{1,0:T(8,128)(2,1)S(1)}, u32[]{:S(2)}, u32[]{:S(2)}) collective-permute-start(bf16[80,488]{1,0:T(8,128)(2,1)S(1)} %pad_maximum_fusion.3), channel_id=1, source_target_pairs={{0,16},{16,0},{4,20},{20,4},{8,24},{24,8},{12,28},{28,12},{32,48},... | collective-permute-start | bytes 234248 | tf_op jit(solution)/shard_map/ppermute | solution.py:18
  32.4 21.5 %copy-start.3 = (s32[1,10,1024]{2,0,1:T(1,128)S(1)}, s32[1,10,1024]{2,0,1:T(1,128)}, u32[]{:S(2)}) copy-start(s32[1,10,1024]{2,0,1:T(1,128)} %param.15) | copy-start | bytes 122884
  32.4 21.5 %copy-start.8 = (s32[1,10]{1,0:T(1,128)S(1)}, s32[1,10]{1,0:T(1,128)}, u32[]{:S(2)}) copy-start(s32[1,10]{1,0:T(1,128)} %param.16) | copy-start | bytes 124
  32.4 22.2 %copy-start.4 = (s32[1,10,1024]{2,0,1:T(1,128)S(1)}, s32[1,10,1024]{2,0,1:T(1,128)}, u32[]{:S(2)}) copy-start(s32[1,10,1024]{2,0,1:T(1,128)} %param.14) | copy-start | bytes 122884
  33.1 4.5 %collective-permute-start.3 = (bf16[80,488]{1,0:T(8,128)(2,1)S(1)}, bf16[80,488]{1,0:T(8,128)(2,1)S(1)}, u32[]{:S(2)}, u32[]{:S(2)}) collective-permute-start(bf16[80,488]{1,0:T(8,128)(2,1)S(1)} %pad_maximum_fusion.4), channel_id=1, source_target_pairs={{0,32},{32,0},{4,36},{36,4},{8,40},{40,8},{12,44},{44,12},{16,48},... | collective-permute-start | bytes 234248 | tf_op jit(solution)/shard_map/ppermute | solution.py:18
  39.0 5.8 %collective-permute-start.4 = (bf16[80,488]{1,0:T(8,128)(2,1)S(1)}, bf16[80,488]{1,0:T(8,128)(2,1)S(1)}, u32[]{:S(2)}, u32[]{:S(2)}) collective-permute-start(bf16[80,488]{1,0:T(8,128)(2,1)S(1)} %pad_maximum_fusion.5), channel_id=1, source_target_pairs={{0,64},{64,0},{4,68},{68,4},{8,72},{72,8},{12,76},{76,12},{16,80},... | collective-permute-start | bytes 234248 | tf_op jit(solution)/shard_map/ppermute | solution.py:18
  46.1 15.7 %collective-permute-start.5 = (bf16[80,488]{1,0:T(8,128)(2,1)S(1)}, bf16[80,488]{1,0:T(8,128)(2,1)S(1)}, u32[]{:S(2)}, u32[]{:S(2)}) collective-permute-start(bf16[80,488]{1,0:T(8,128)(2,1)S(1)} %pad_maximum_fusion.6), channel_id=1, source_target_pairs={{0,128},{128,0},{4,132},{132,4},{8,136},{136,8},{12,140},{140,12},... | collective-permute-start | bytes 234248 | tf_op jit(solution)/shard_map/ppermute | solution.py:18
  55.3 43.7 %reduce-scatter.5.cloned.1.call-start = ((), (), s32[]{:S(2)}) async-start(), calls=%async_computation.4 | async-start | bytes 655360 | tf_op jit(solution)/shard_map/reduce_scatter | solution.py:154
  61.9 2.4 %copy-start = (bf16[10,488,488]{2,1,0:T(8,128)(2,1)S(1)}, bf16[10,488,488]{2,1,0:T(8,128)(2,1)}, u32[]{:S(2)}) copy-start(bf16[10,488,488]{2,1,0:T(8,128)(2,1)} %k_ref.9) | copy-start | bytes 14288644
  77.3 47.9 %reduce-scatter.7.cloned.1.call-start = ((), (), s32[]{:S(2)}) async-start(), calls=%async_computation.5 | async-start | bytes 655360 | tf_op jit(solution)/shard_map/reduce_scatter | solution.py:154
  99.0 52.2 %reduce-scatter.9.cloned.1.call-start = ((), (), s32[]{:S(2)}) async-start(), calls=%async_computation.6 | async-start | bytes 655360 | tf_op jit(solution)/shard_map/reduce_scatter | solution.py:154
  125.2 52.2 %copy-start.1 = (f32[64,488]{1,0:T(8,128)S(1)}, f32[64,488]{1,0:T(8,128)}, u32[]{:S(2)}) copy-start(f32[64,488]{1,0:T(8,128)} %reduce-scatter.5.cloned.1.call-done) | copy-start | bytes 374788
  125.2 52.2 %copy-start.2 = (f32[64,488]{1,0:T(8,128)S(1)}, f32[64,488]{1,0:T(8,128)}, u32[]{:S(2)}) copy-start(f32[64,488]{1,0:T(8,128)} %reduce-scatter.7.cloned.1.call-done) | copy-start | bytes 374788
  125.2 52.2 %reduce-scatter.11.cloned.1.call-start = ((), (), s32[]{:S(2)}) async-start(), calls=%async_computation.7 | async-start | bytes 655360 | tf_op jit(solution)/shard_map/reduce_scatter | solution.py:154
Sparse Core Ops, SparseCore 0:
  18.1 2.2 sort.39.cloned.1.call-done
  55.4 4.3 sort.37.cloned.1.call-done
  77.4 21.5 reduce-scatter.4
  101.4 23.7 reduce-scatter.6
  127.5 23.6 reduce-scatter.8
  153.6 23.7 reduce-scatter.10
  (2 shorter events, 0.0 us)
